TPU v7x, 32 devices: a whole 2x2x4 slice. The times are simulated.
32 devices in a mesh: dp: 8 (over y, x, core), mp: 4 (over z).
Axes of the slice: x: 2, y: 2, z: 4, core: 2. Of those that a mesh axis runs over, the one named last changes fastest.
Arguments:
- tokens: bfloat16 [8192, 5120], P('dp'), may hold values from -6 to 6
- norm_gain: bfloat16 [5120], replicated, may hold values from 0.099609375 to 1.8984375
- w_query: bfloat16 [5120, 5120], P('dp', 'mp'), may hold values from -0.078125 to 0.078125
- b_query: bfloat16 [5120], P('mp'), may hold values from -3 to 3
- keyvalue_weight: bfloat16 [5120, 2, 1024], P('dp', None, 'mp'), may hold values from -0.078125 to 0.078125
- b_keyval: bfloat16 [2, 1024], P(None, 'mp'), may hold values from -3 to 3
- w_out: bfloat16 [5120, 5120], P('mp', 'dp'), may hold values from -0.5 to 0.5
- kv_pool: bfloat16 [2, 512, 64, 1024], P(None, 'dp', None, 'mp'), may hold values from -64 to 64
- page_owner: int32 [8, 16], replicated, may hold values from 0 to 7, as said below
- page_index: int32 [8, 16], replicated, may hold values from 0 to 63
- prefix_pages: int32 [8], replicated, may hold values from 10 to 16, as said below
- prompt_device: int32 [8], replicated, may hold values from 0 to 7, each once
Outputs:
- attn_out: bfloat16 [8192, 5120], P('dp', 'mp')
Inputs may be any that keep to these rules, and one draw needn't show every extreme that they name: `page_owner`: slots at or beyond a prompt's prefix_pages are unused. Of one prompt's used slots at most 2 name the same owner, and some prompt has exactly 2 used slots with one owner. `prefix_pages`: some prompt has 16 used slots.
All inputs are finite; a program needn't handle non-finite values.
Results may differ from a plain program's by a relative error of at most 0.014.
The roundings to bfloat16 on the way count: a program that leaves them out, or rounds other values in their place, can miss the bound.
Values may be sent and summed in bfloat16 or wider, within the bound.
A program may use at most 192 MiB of HBM per device.

v0:
```python
import functools
import math

import jax
import jax.numpy as jnp
from jax import lax
from jax.experimental import pallas as pl
from jax.experimental.pallas import tpu as pltpu
from jax.sharding import PartitionSpec as P


HD = 128
CAP = 2
ROW_PARTS = 2


rope_theta = 1000000.0
norm_eps = 1e-06
masked_score = -1e30


def rms_normed(rows, norm_gain):
    values = rows.astype(jnp.float32)
    inverse = lax.rsqrt(jnp.mean(values * values, axis=-1, keepdims=True) + norm_eps)
    return (values * inverse * norm_gain.astype(jnp.float32)).astype(jnp.bfloat16)


def rotary_tables(positions):
    half_dim = HD // 2
    frequency = rope_theta ** (-jnp.arange(half_dim, dtype=jnp.float32) * 2.0 / HD)
    angles = positions.astype(jnp.float32)[:, None] * frequency[None, :]
    cosine = jnp.cos(angles)
    sine = jnp.sin(angles)
    return (
        jnp.concatenate([cosine, cosine], axis=-1),
        jnp.concatenate([-sine, sine], axis=-1),
    )


def attention_kernel(block, prev_len, *refs):
    q_ref, k_ref, v_ref, cos_ref, sin_ref, bias_ref, kp_ref, vp_ref = refs[:8]
    refs = refs[8:]
    if prev_len:
        k_prev_ref, v_prev_ref = refs[:2]
        refs = refs[2:]
    o_ref, k_out, v_out = refs
    cosine = cos_ref[...]
    sine = sin_ref[...]

    def rotate(x):
        return (x * cosine + pltpu.roll(x, HD // 2, 1) * sine).astype(jnp.bfloat16)

    @pl.when(pl.program_id(0) == 0)
    def _():
        k_out[...] = rotate(k_ref[...])
        v_out[...] = v_ref[...].astype(jnp.bfloat16)

    query = rotate(q_ref[...])
    factor = HD ** (-0.5) * math.log2(math.e)
    rows = query.shape[0]
    ids = lax.broadcasted_iota(jnp.int32, (block, block), 0)
    keys_id = lax.broadcasted_iota(jnp.int32, (block, block), 1)

    def scores(q, k):
        return lax.dot_general(q, k, (((1,), (1,)), ((), ())), preferred_element_type=jnp.float32)

    for begin in range(0, rows, block):
        q = query[begin : begin + block]
        parts = [(scores(q, kp_ref[0]) + bias_ref[...], vp_ref[0])]
        if prev_len:
            parts.append((scores(q, k_prev_ref[...]), v_prev_ref[...]))
        if begin:
            parts.append((scores(q, k_out[0:begin, :]), v_out[0:begin, :]))
        diagonal = scores(q, k_out[begin : begin + block, :])
        diagonal = jnp.where(keys_id <= ids, diagonal, masked_score)
        parts.append((diagonal, v_out[begin : begin + block, :]))
        top = functools.reduce(
            jnp.maximum, [jnp.max(s, axis=-1, keepdims=True) for s, _ in parts]
        )
        total = None
        out = None
        for s, v in parts:
            raised = jnp.exp2((s - top) * factor)
            row_sum = jnp.sum(raised, axis=-1, keepdims=True)
            term = jnp.dot(raised.astype(jnp.bfloat16), v, preferred_element_type=jnp.float32)
            total = row_sum if total is None else total + row_sum
            out = term if out is None else out + term
        o_ref[begin : begin + block, :] = (out / total).astype(jnp.bfloat16)


def attention(group, qkv, cosine, sine, bias, arrived, prev, per_group):
    rows = qkv.shape[0]
    cached_len = arrived.shape[1]
    block = math.gcd(256, rows)
    const = lambda shape, index: pl.BlockSpec(shape, lambda h: index)
    in_specs = [
        pl.BlockSpec((rows, HD), lambda h: (0, h)),
        const((rows, HD), (0, per_group)),
        const((rows, HD), (0, per_group + 1)),
        const((rows, HD), (0, 0)),
        const((rows, HD), (0, 0)),
        const((1, cached_len), (0, 0)),
        const((1, cached_len, HD), (0, 0, group)),
        const((1, cached_len, HD), (1, 0, group)),
    ]
    operands = [qkv, qkv, qkv, cosine, sine, bias, arrived, arrived]
    prev_len = 0
    if prev is not None:
        prev_len = prev[0].shape[0]
        in_specs += [const((prev_len, HD), (0, 0))] * 2
        operands += list(prev)
    keys = cached_len + prev_len + rows
    return pl.pallas_call(
        functools.partial(attention_kernel, block, prev_len),
        grid=(per_group,),
        in_specs=in_specs,
        out_specs=[
            pl.BlockSpec((rows, HD), lambda h: (0, h)),
            const((rows, HD), (0, 0)),
            const((rows, HD), (0, 0)),
        ],
        out_shape=[
            jax.ShapeDtypeStruct((rows, per_group * HD), jnp.bfloat16),
            jax.ShapeDtypeStruct((rows, HD), jnp.bfloat16),
            jax.ShapeDtypeStruct((rows, HD), jnp.bfloat16),
        ],
        compiler_params=pltpu.CompilerParams(
            dimension_semantics=("arbitrary",), vmem_limit_bytes=40 * 1024 * 1024
        ),
        cost_estimate=pl.CostEstimate(
            flops=8 * per_group * rows * keys * HD,
            bytes_accessed=6 * rows * (per_group + 2) * HD,
            transcendentals=per_group * rows * keys,
        ),
    )(*operands)


def exchange(x, axis, split_axis, concat_axis):
    size = lax.axis_size(axis)
    me = lax.axis_index(axis)
    width = x.shape[split_axis] // size
    span = x.shape[concat_axis]
    shape = list(x.shape)
    shape[split_axis] = width
    shape[concat_axis] = span * size
    result = jnp.zeros(shape, x.dtype)
    for s in range(size):
        target = lax.rem(me + s, size)
        source = lax.rem(me - s + size, size)
        piece = lax.dynamic_slice_in_dim(x, target * width, width, split_axis)
        if s:
            piece = lax.ppermute(piece, axis, [(i, (i + s) % size) for i in range(size)])
        result = lax.dynamic_update_slice_in_dim(result, piece, source * span, concat_axis)
    return result


def shards(*arguments):
    kv_local = arguments[4].shape[2] // HD
    if square_mesh() and kv_local == 2:
        return fused_layer(*arguments)
    return layer(*arguments)


def square_mesh():
    return lax.axis_size("dp") == 8 and lax.axis_size("mp") == 4


def layer(
    tokens,
    norm_gain,
    w_query,
    b_query,
    keyvalue_weight,
    b_keyval,
    w_out,
    kv_pool,
    page_owner,
    page_index,
    prefix_pages,
    prompt_device,
):
    groups = lax.axis_size("dp")
    planes = lax.axis_size("mp")
    my_group = lax.axis_index("dp")
    my_plane = lax.axis_index("mp")
    seq_rows = tokens.shape[0]
    width_kv = keyvalue_weight.shape[2]
    kv_local = width_kv // HD
    heads_local = w_query.shape[1] // HD
    per_group = heads_local // kv_local
    page_len = kv_pool.shape[2]
    max_pages = page_owner.shape[1]
    group_ids = jnp.arange(groups, dtype=jnp.int32)

    width_q = per_group * HD
    gathered = []
    biases = []
    for g in range(kv_local):
        piece = jnp.concatenate(
            [
                w_query[:, g * width_q : (g + 1) * width_q],
                keyvalue_weight[:, 0, g * HD : (g + 1) * HD],
                keyvalue_weight[:, 1, g * HD : (g + 1) * HD],
            ],
            axis=1,
        )
        gathered.append(lax.all_gather(piece, "dp", axis=0, tiled=True))
        biases.append(
            jnp.concatenate(
                [
                    b_query[g * width_q : (g + 1) * width_q],
                    b_keyval[0, g * HD : (g + 1) * HD],
                    b_keyval[1, g * HD : (g + 1) * HD],
                ]
            ).astype(jnp.float32)
        )

    slot_prompt = jnp.sum(
        jnp.where(prompt_device[None, :] == group_ids[:, None], group_ids[None, :], 0), axis=1
    )
    owners_all = jnp.take(page_owner, slot_prompt, axis=0)
    index_all = jnp.take(page_index, slot_prompt, axis=0)
    length_all = jnp.take(prefix_pages, slot_prompt, axis=0)
    slot_ids = jnp.arange(max_pages, dtype=jnp.int32)
    places = jnp.arange(CAP, dtype=jnp.int32)
    used = slot_ids[None, :] < length_all[:, None]
    mine = used & (owners_all == my_group)
    rank = jnp.cumsum(mine.astype(jnp.int32), axis=1) - 1
    chosen = mine[:, None, :] & (rank[:, None, :] == places[None, :, None])
    send_index = jnp.sum(jnp.where(chosen, index_all[:, None, :], 0), axis=2)
    outgoing = jnp.take(kv_pool, send_index.reshape(-1), axis=1).reshape(
        2, groups, CAP, page_len, width_kv
    )
    arrived = lax.all_to_all(outgoing, "dp", split_axis=1, concat_axis=1, tiled=True)
    my_owners = jnp.take(owners_all, my_group, axis=0)
    my_length = jnp.take(length_all, my_group, axis=0)
    my_used = slot_ids < my_length
    counts = jnp.sum(
        ((my_owners[None, :] == group_ids[:, None]) & my_used[None, :]).astype(jnp.int32), axis=1
    )
    page_live = (places[None, :] < counts[:, None]).reshape(-1)
    cached_len = page_live.shape[0] * page_len
    arrived = arrived.reshape(2, cached_len, width_kv)
    bias = jnp.where(jnp.repeat(page_live, page_len), 0.0, masked_score).astype(jnp.float32)[None]

    normed = rms_normed(tokens, norm_gain)
    arrived, w_out = lax.optimization_barrier((arrived, w_out))
    out_rows = exchange(w_out, "dp", 0, 1)
    out_rows = exchange(out_rows, "mp", 1, 0)
    out_weight = lax.all_gather(out_rows, "dp", axis=0, tiled=True)
    out_cols = out_weight.shape[1]
    out_weight = out_weight.reshape(groups, planes, -1, out_cols)
    cosine, sine = rotary_tables(
        my_length * page_len + jnp.arange(seq_rows, dtype=jnp.int32)
    )
    part = seq_rows // ROW_PARTS
    held = [[[] for _ in range(ROW_PARTS)] for _ in range(planes)]
    for g in range(kv_local):
        prev = None
        for r in range(ROW_PARTS):
            rows = slice(r * part, (r + 1) * part)
            qkv = (
                jnp.dot(normed[rows], gathered[g], preferred_element_type=jnp.float32)
                + biases[g]
            )
            attended, keys, values = attention(
                g, qkv, cosine[rows], sine[rows], bias, arrived, prev, per_group
            )
            if prev is None:
                prev = (keys, values)
            else:
                prev = (
                    jnp.concatenate([prev[0], keys], axis=0),
                    jnp.concatenate([prev[1], values], axis=0),
                )
            held[0][r].append(attended)
            for s in range(1, planes):
                high = 1 << (s.bit_length() - 1)
                low = s - high
                _, moved, step = ("relay", held[high][r][g], low) if low else ("send", attended, s)
                held[s][r].append(lax.ppermute(moved, "mp", [(i, i ^ step) for i in range(planes)]))
    weights = []
    for s in range(planes):
        source = my_plane ^ s
        rows_of = lax.dynamic_index_in_dim(out_weight, source, axis=1, keepdims=False)
        weights.append(rows_of.reshape(-1, out_cols))
    outputs = []
    for r in range(ROW_PARTS):
        total = None
        for s in range(planes):
            head_partial = None
            for g in range(kv_local):
                term = jnp.dot(
                    held[s][r][g],
                    weights[s][g * width_q : (g + 1) * width_q],
                    preferred_element_type=jnp.float32,
                )
                head_partial = term if head_partial is None else term + head_partial
            head_partial = head_partial.astype(jnp.bfloat16).astype(jnp.float32)
            total = head_partial if total is None else total + head_partial
        outputs.append(total.astype(jnp.bfloat16))
    return jnp.concatenate(outputs, axis=0)


MESH = pl.DeviceIdType.MESH
BLOCK = 256
TILE = 2 * HD
X, Y, FAR, OWN, OX, OY, OFAR = range(7)


def fused_kernel(
    tokens, w_query, w_keyval, w_out, outgoing, gain, bias, mask, cosine, sine,
    out, relay,
    normed, wqkv, wout, cache, keys, values, query, att, att_in, part_in,
    token_sem, own_sem, send_sem, recv_sem, page_send, page_recv, page_own,
    z_send, z_recv, part_send, part_recv, move_send, move_recv, out_sem,
):
    div, rem = lax.div, lax.rem
    groups = lax.axis_size("dp")
    planes = lax.axis_size("mp")
    d = lax.axis_index("dp")
    m = lax.axis_index("mp")
    rows = tokens.shape[0]
    half_rows = rows // 2
    blocks = rows // BLOCK
    depth = w_query.shape[0]
    q_width = w_query.shape[1]
    tiles = q_width // TILE
    kv_chunks = w_keyval.shape[1] // TILE
    per_group = q_width // HD // kv_chunks
    chunks = kv_chunks + tiles
    out_depth, out_cols = w_out.shape
    out_parts = 2
    part_depth = out_depth // out_parts

    core = rem(d, 2)
    x_bit = rem(div(d, 2), 2)
    y_bit = rem(div(d, 4), 2)
    core_n = d + 1 - 2 * core
    x_n = d + 2 - 4 * x_bit
    y_n = d + 4 - 8 * y_bit
    far = x_n + y_n - d
    far_src = x_n + core * (y_n - x_n)
    far_dst = y_n + core * (x_n - y_n)

    def piece(k, owner):
        if isinstance(k, int) and k >= chunks:
            return wout.at[owner, pl.ds((k - chunks) * part_depth, part_depth), :]
        return wqkv.at[
            pl.ds(pl.multiple_of(owner * depth, depth), depth),
            pl.ds(pl.multiple_of(k * TILE, TILE), TILE),
        ]

    routes = {
        X: (d, x_n),
        Y: (d, y_n),
        FAR: (far_src, far_dst),
        OWN: (d, core_n),
        OX: (x_n, core_n),
        OY: (y_n, core_n),
        OFAR: (far, core_n),
    }

    def hop(kind, k):
        owner, target = routes[kind]
        region = piece(k, owner)
        return pltpu.make_async_remote_copy(
            src_ref=region,
            dst_ref=region,
            send_sem=send_sem.at[kind, k],
            recv_sem=recv_sem.at[kind, k],
            device_id=(target, m),
            device_id_type=MESH,
        )

    def issue(k):
        for kind in (X, Y, OWN):
            hop(kind, k).start()

    def forward(k):
        hop(X, k).wait_recv()
        hop(Y, k).wait_recv()
        for kind in (FAR, OX, OY):
            hop(kind, k).start()

    def complete(k):
        hop(FAR, k).wait_recv()
        hop(OFAR, k).start()
        for kind in (OWN, OX, OY, OFAR):
            hop(kind, k).wait_recv()

    barrier = pltpu.get_barrier_semaphore()
    for s in range(1, groups):
        pl.semaphore_signal(
            barrier, inc=1, device_id=(rem(d + s, groups), m), device_id_type=MESH
        )
    for s in range(1, planes):
        pl.semaphore_signal(
            barrier, inc=1, device_id=(d, rem(m + s, planes)), device_id_type=MESH
        )

    def own_copy(k):
        if k < kv_chunks:
            source = w_keyval.at[:, pl.ds(k * TILE, TILE)]
        else:
            source = w_query.at[:, pl.ds((k - kv_chunks) * TILE, TILE)]
        return pltpu.make_async_copy(source, piece(k, d), own_sem.at[k])

    for k in range(chunks):
        own_copy(k).start()

    def token_copy(b):
        part = pl.ds(b * BLOCK, BLOCK)
        return pltpu.make_async_copy(tokens.at[part, :], normed.at[part, :], token_sem.at[b])

    for b in range(blocks):
        token_copy(b).start()
    page_local = pltpu.make_async_copy(outgoing.at[:, d], cache.at[:, d], page_own)
    page_local.start()

    pl.semaphore_wait(barrier, groups + planes - 2)

    def page_copy(s):
        target = rem(d + s, groups)
        return pltpu.make_async_remote_copy(
            src_ref=outgoing.at[:, target],
            dst_ref=cache.at[:, d],
            send_sem=page_send.at[s - 1],
            recv_sem=page_recv.at[s - 1],
            device_id=(target, m),
            device_id_type=MESH,
        )

    ahead = 3
    for k in range(ahead):
        own_copy(k).wait()
        issue(k)
        if k == 0:
            for s in range(1, groups):
                page_copy(s).start()
    for k in range(ahead, chunks):
        own_copy(k).wait()

    odd = rem(m, 2)
    side = div(m, 2)
    upper = rem(y_bit + m, 2)
    plane_to = 2 * upper + side

    def swap_copy():
        return pltpu.make_async_remote_copy(
            src_ref=w_out,
            dst_ref=relay,
            send_sem=move_send.at[0],
            recv_sem=move_recv.at[0],
            device_id=(y_n, m),
            device_id_type=MESH,
        )

    def lift_copy(source):
        return pltpu.make_async_remote_copy(
            src_ref=source,
            dst_ref=wout.at[d],
            send_sem=move_send.at[1],
            recv_sem=move_recv.at[1],
            device_id=(d, plane_to),
            device_id_type=MESH,
        )

    def stay_copy(source):
        return pltpu.make_async_copy(source, wout.at[d], move_recv.at[1])

    @pl.when(odd == 1)
    def _():
        swap_copy().start()

    @pl.when((odd == 0) & (plane_to == m))
    def _():
        stay_copy(w_out).start()

    @pl.when((odd == 0) & (plane_to != m))
    def _():
        lift_copy(w_out).start()

    step_rows = 16

    def normalize(first, count):
        def body(i, carry):
            part = pl.ds(pl.multiple_of(first + i * step_rows, step_rows), step_rows)
            value = normed[part, :].astype(jnp.float32)
            inverse = lax.rsqrt(jnp.mean(value * value, axis=-1, keepdims=True) + norm_eps)
            normed[part, :] = (value * inverse * gain[...]).astype(jnp.bfloat16)
            return carry

        lax.fori_loop(0, count // step_rows, body, 0)

    for b in range(blocks // 2):
        token_copy(b).wait()
        normalize(b * BLOCK, BLOCK)
    forward(0)
    issue(ahead)
    for b in range(blocks // 2, blocks):
        token_copy(b).wait()
        normalize(b * BLOCK, BLOCK)

    @pl.when(odd == 1)
    def _():
        swap_copy().wait_recv()

    @pl.when((odd == 1) & (plane_to == m))
    def _():
        stay_copy(relay).start()

    @pl.when((odd == 1) & (plane_to != m))
    def _():
        lift_copy(relay).start()

    complete(0)
    forward(1)
    issue(ahead + 1)

    def project(first, k):
        columns = pl.ds(pl.multiple_of(k * TILE, TILE), TILE)
        result = jnp.dot(
            normed[first : first + half_rows, :],
            wqkv[:, columns],
            preferred_element_type=jnp.float32,
        )
        return result + bias[:, columns]

    def rotate(x, first):
        part = slice(first, first + half_rows)
        return (x * cosine[part, :] + pltpu.roll(x, HD // 2, 1) * sine[part, :]).astype(
            jnp.bfloat16
        )

    def project_keyval(g):
        for first in (0, half_rows):
            x = project(first, g)
            keys[first : first + half_rows, g * HD : (g + 1) * HD] = rotate(x[:, :HD], first)
            values[first : first + half_rows, g * HD : (g + 1) * HD] = x[:, HD:].astype(
                jnp.bfloat16
            )

    project_keyval(0)
    forward(2)
    issue(ahead + 2)
    complete(1)
    project_keyval(1)
    for s in range(1, groups):
        page_copy(s).wait_recv()
    page_local.wait()

    factor = HD ** (-0.5) * math.log2(math.e)
    cached_len = groups * cache.shape[2]

    def scores(q, k):
        return lax.dot_general(q, k, (((1,), (1,)), ((), ())), preferred_element_type=jnp.float32)

    def attend(first, t):
        x = project(first, kv_chunks + t)
        for j in range(2):
            query[:, j * HD : (j + 1) * HD] = rotate(x[:, j * HD : (j + 1) * HD], first)

        def head(j, carry):
            mine = pl.ds(pl.multiple_of(j * HD, HD), HD)
            group = div(2 * t + j, per_group)
            own = pl.ds(pl.multiple_of(group * HD, HD), HD)
            target = pl.ds(pl.multiple_of(t * TILE + j * HD, HD), HD)
            old_keys = cache[0, :, :, own].reshape(cached_len, HD)
            old_values = cache[1, :, :, own].reshape(cached_len, HD)
            for begin in range(first, first + half_rows, BLOCK):
                q = query[begin - first : begin - first + BLOCK, mine]
                parts = [(scores(q, old_keys) + mask[...], old_values)]
                if begin:
                    parts.append((scores(q, keys[0:begin, own]), values[0:begin, own]))
                diagonal = scores(q, keys[begin : begin + BLOCK, own])
                row_id = lax.broadcasted_iota(jnp.int32, (BLOCK, BLOCK), 0)
                key_id = lax.broadcasted_iota(jnp.int32, (BLOCK, BLOCK), 1)
                diagonal = jnp.where(key_id <= row_id, diagonal, masked_score)
                parts.append((diagonal, values[begin : begin + BLOCK, own]))
                top = functools.reduce(
                    jnp.maximum, [jnp.max(s, axis=-1, keepdims=True) for s, _ in parts]
                )
                total = None
                result = None
                for s, v in parts:
                    raised = jnp.exp2((s - top) * factor)
                    row_sum = jnp.sum(raised, axis=-1, keepdims=True)
                    term = jnp.dot(
                        raised.astype(jnp.bfloat16), v, preferred_element_type=jnp.float32
                    )
                    total = row_sum if total is None else total + row_sum
                    result = term if result is None else result + term
                att[begin : begin + BLOCK, target] = (result / total).astype(jnp.bfloat16)
            return carry

        lax.fori_loop(0, 2, head, 0)

    slot = odd
    primary = 2 - side
    secondary = 3 * side

    def attended_part(i):
        if isinstance(i, int) and i >= tiles:
            return pl.ds(half_rows + (i - tiles) * BLOCK, BLOCK), pl.ds(0, q_width)
        return pl.ds(0, half_rows), pl.ds(pl.multiple_of(i * TILE, TILE), TILE)

    def z_copy(which, i):
        part, columns = attended_part(i)
        return pltpu.make_async_remote_copy(
            src_ref=att.at[part, columns],
            dst_ref=att_in.at[slot, part, columns],
            send_sem=z_send.at[which, i],
            recv_sem=z_recv.at[slot, i],
            device_id=(d, secondary if which else primary),
            device_id_type=MESH,
        )

    def z_keep(i):
        part, columns = attended_part(i)
        return pltpu.make_async_copy(
            att.at[part, columns], att_in.at[slot, part, columns], z_recv.at[slot, i]
        )

    def z_start(i):
        z_copy(0, i).start()

        @pl.when(m != secondary)
        def _():
            z_copy(1, i).start()

        @pl.when(m == secondary)
        def _():
            z_keep(i).start()

    def z_wait(i):
        part, columns = attended_part(i)
        for s in range(2):
            pltpu.make_async_copy(
                att.at[part, columns], att_in.at[s, part, columns], z_recv.at[s, i]
            ).wait()

    def tile_step(t, carry):
        k = t + kv_chunks
        complete(k)
        attend(0, t)
        z_start(t)

        @pl.when(t < tiles - 1)
        def _():
            forward(k + 1)

        @pl.when(t < tiles - 2)
        def _():
            issue_ahead = k + 2

            @pl.when(issue_ahead >= 2 * ahead)
            def _():
                issue(issue_ahead)

        @pl.when(t == tiles - 2)
        def _():
            stay_copy(relay).wait()
            for part in range(out_parts):
                issue(chunks + part)

        attend(half_rows, t)
        return carry

    lax.fori_loop(0, tiles, tile_step, 0)
    for i in range(tiles, tiles + blocks // 2):
        z_start(i)
    for part in range(out_parts):
        forward(chunks + part)
    for part in range(out_parts):
        complete(chunks + part)

    partner = m + 1 - 2 * odd

    def part_copy(b):
        part = pl.ds(b * BLOCK, BLOCK)
        return pltpu.make_async_remote_copy(
            src_ref=normed.at[part, pl.ds(0, q_width)],
            dst_ref=part_in.at[part, :],
            send_sem=part_send.at[b],
            recv_sem=part_recv.at[b],
            device_id=(d, partner),
            device_id_type=MESH,
        )

    def head_partial(b, q, column_block):
        total = None
        for j in range(2):
            order = j + side * 0 + upper_side * (1 - 2 * j)
            index = order * (groups // 2) + column_block * 2 + q
            term = jnp.dot(
                att_in[j, b * BLOCK : (b + 1) * BLOCK, :],
                wout[index],
                preferred_element_type=jnp.float32,
            )
            total = term if total is None else total + term
        return total

    upper_side = div(m, 2)

    def send_partial(b):
        for q in range(2):
            normed[b * BLOCK : (b + 1) * BLOCK, q * out_cols : (q + 1) * out_cols] = head_partial(
                b, q, 1 - odd
            ).astype(jnp.bfloat16)
        part_copy(b).start()

    def out_copy(b):
        part = pl.ds(b * BLOCK, BLOCK)
        return pltpu.make_async_copy(
            normed.at[part, pl.ds(q_width, q_width)], out.at[part, :], out_sem.at[b]
        )

    def finish(b):
        mine = [head_partial(b, q, odd) for q in range(2)]
        part_copy(b).wait_recv()
        for q in range(2):
            columns = slice(q * out_cols, (q + 1) * out_cols)
            normed[
                b * BLOCK : (b + 1) * BLOCK, q_width + q * out_cols : q_width + (q + 1) * out_cols
            ] = (
                mine[q] + part_in[b * BLOCK : (b + 1) * BLOCK, columns].astype(jnp.float32)
            ).astype(jnp.bfloat16)
        out_copy(b).start()

    for i in range(tiles):
        z_wait(i)
    for b in range(blocks // 2):
        send_partial(b)
    for b in range(blocks // 2, blocks):
        z_wait(tiles + b - blocks // 2)
        send_partial(b)
    for b in range(blocks):
        finish(b)

    for k in range(chunks + out_parts):
        for kind in routes:
            hop(kind, k).wait_send()
    for s in range(1, groups):
        page_copy(s).wait_send()

    @pl.when(odd == 1)
    def _():
        swap_copy().wait_send()

    @pl.when(plane_to != m)
    def _():
        lift_copy(w_out).wait_send()

    for i in range(tiles + blocks // 2):
        z_copy(0, i).wait_send()

        @pl.when(m != secondary)
        def _():
            z_copy(1, i).wait_send()

    for b in range(blocks):
        part_copy(b).wait_send()
        out_copy(b).wait()


def fused_layer(tokens, norm_gain, w_query, b_query, keyvalue_weight, b_keyval, w_out, kv_pool,
                page_owner, page_index, prefix_pages, prompt_device):
    groups = lax.axis_size("dp")
    my_group = lax.axis_index("dp")
    rows, features = tokens.shape
    _, q_width = w_query.shape
    width_kv = keyvalue_weight.shape[2]
    kv_local = width_kv // HD
    page_len = kv_pool.shape[2]
    group_ids = jnp.arange(groups, dtype=jnp.int32)

    plan = page_plan(
        kv_pool, page_owner, page_index, prefix_pages, prompt_device, groups, my_group
    )
    outgoing, bias, my_length = plan
    outgoing = outgoing.reshape(2, groups, CAP * page_len, width_kv)
    cosine, sine = rotary_tables(my_length * page_len + jnp.arange(rows, dtype=jnp.int32))

    def interleave(x):
        return jnp.swapaxes(x.reshape(x.shape[0], 2, kv_local, HD), 1, 2).reshape(x.shape[0], -1)

    w_keyval = interleave(keyvalue_weight)
    bias_row = jnp.concatenate([interleave(b_keyval[None])[0], b_query]).astype(jnp.float32)[None]
    gain = norm_gain.astype(jnp.float32)[None]
    any_spec = pl.BlockSpec(memory_space=pl.ANY)
    vmem = pl.BlockSpec(memory_space=pltpu.VMEM)
    tiles = q_width // (2 * HD)
    chunks = tiles + kv_local
    out_parts = 2
    blocks = rows // BLOCK
    sends = tiles + blocks // 2
    dma = pltpu.SemaphoreType.DMA
    bf16 = jnp.bfloat16
    out, _ = pl.pallas_call(
        fused_kernel,
        in_specs=[any_spec] * 5 + [vmem] * 5,
        out_specs=[any_spec, any_spec],
        out_shape=[
            jax.ShapeDtypeStruct((rows, 2 * w_out.shape[1]), bf16),
            jax.ShapeDtypeStruct(w_out.shape, bf16),
        ],
        scratch_shapes=[
            pltpu.VMEM((rows, features), bf16),
            pltpu.VMEM((features, q_width + 2 * width_kv), bf16),
            pltpu.VMEM((groups,) + w_out.shape, bf16),
            pltpu.VMEM((2, groups, CAP * page_len, width_kv), bf16),
            pltpu.VMEM((rows, width_kv), bf16),
            pltpu.VMEM((rows, width_kv), bf16),
            pltpu.VMEM((rows // 2, 2 * HD), bf16),
            pltpu.VMEM((rows, q_width), bf16),
            pltpu.VMEM((2, rows, q_width), bf16),
            pltpu.VMEM((rows, q_width), bf16),
            dma((blocks,)),
            dma((chunks,)),
            dma((7, chunks + out_parts)),
            dma((7, chunks + out_parts)),
            dma((groups - 1,)),
            dma((groups - 1,)),
            dma,
            dma((2, sends)),
            dma((2, sends)),
            dma((blocks,)),
            dma((blocks,)),
            dma((2,)),
            dma((2,)),
            dma((blocks,)),
        ],
        compiler_params=pltpu.CompilerParams(
            collective_id=0, has_side_effects=True, vmem_limit_bytes=67000000
        ),
    )(tokens, w_query, w_keyval, w_out, outgoing, gain, bias_row, bias, cosine, sine)
    return out


def page_plan(kv_pool, page_owner, page_index, prefix_pages, prompt_device, groups, my_group):
    width_kv = kv_pool.shape[3]
    page_len = kv_pool.shape[2]
    max_pages = page_owner.shape[1]
    group_ids = jnp.arange(groups, dtype=jnp.int32)
    slot_prompt = jnp.sum(
        jnp.where(prompt_device[None, :] == group_ids[:, None], group_ids[None, :], 0), axis=1
    )
    owners_all = jnp.take(page_owner, slot_prompt, axis=0)
    index_all = jnp.take(page_index, slot_prompt, axis=0)
    length_all = jnp.take(prefix_pages, slot_prompt, axis=0)
    slot_ids = jnp.arange(max_pages, dtype=jnp.int32)
    places = jnp.arange(CAP, dtype=jnp.int32)
    used = slot_ids[None, :] < length_all[:, None]
    mine = used & (owners_all == my_group)
    rank = jnp.cumsum(mine.astype(jnp.int32), axis=1) - 1
    chosen = mine[:, None, :] & (rank[:, None, :] == places[None, :, None])
    send_index = jnp.sum(jnp.where(chosen, index_all[:, None, :], 0), axis=2)
    outgoing = jnp.take(kv_pool, send_index.reshape(-1), axis=1).reshape(
        2, groups, CAP, page_len, width_kv
    )
    my_owners = jnp.take(owners_all, my_group, axis=0)
    my_length = jnp.take(length_all, my_group, axis=0)
    my_used = slot_ids < my_length
    counts = jnp.sum(
        ((my_owners[None, :] == group_ids[:, None]) & my_used[None, :]).astype(jnp.int32), axis=1
    )
    page_live = (places[None, :] < counts[:, None]).reshape(-1)
    bias = jnp.where(jnp.repeat(page_live, page_len), 0.0, masked_score).astype(jnp.float32)[None]
    return outgoing, bias, my_length


def solution(mesh):
    return jax.shard_map(
        shards,
        mesh=mesh,
        in_specs=(
            P("dp", None),
            P(),
            P("dp", "mp"),
            P("mp"),
            P("dp", None, "mp"),
            P(None, "mp"),
            P("mp", "dp"),
            P(None, "dp", None, "mp"),
            P(),
            P(),
            P(),
            P(),
        ),
        out_specs=P("dp", "mp"),
        check_vma=False,
    )
```

profile of v0, /device:TPU:24, one launch (start us, length us, event | category | flops | bytes accessed | tf_op | source)
XLA Modules:
  0.0 306.5 jit_solution(1119626846009738993)
XLA Ops:
  0.0 0.0 copy-start
  0.0 0.8 select_reduce_fusion.1
  0.8 0.7 concatenate.20
  1.5 1.3 gather_fusion
  2.8 0.6 dynamic-slice.6
  4.1 0.6 gather_fusion.3
  4.7 1.2 gather_fusion.2
  5.9 0.1 fusion.8
  6.0 0.1 convert_reduce_fusion
  6.1 0.2 reduce_window_sum.11
  6.3 0.1 broadcast_select_fusion
  6.4 0.1 select_reduce_fusion
  6.5 0.1 copy.20
  6.6 0.1 broadcast_in_dim.97
  6.7 0.1 broadcast_in_dim.98
  6.8 0.1 copy.21
  6.9 0.1 reshape.161
  7.0 0.1 fusion.3
  7.1 0.1 select_n.112
  7.1 0.7 concatenate.21
  7.8 0.6 maximum_convert_fusion.bias
  8.4 0.1 broadcast_in_dim.107
  8.5 0.7 select_n.113.mask
  9.2 1.3 broadcast_in_dim.111
  10.5 2.8 reshape.160.w_keyval
  13.3 2.8 gather_fusion.1
  16.1 0.1 copy.22
  16.2 1.2 bitcast_select_fusion.outgoing
  17.4 1.9 fusion
  19.3 1.3 pad_maximum_fusion
  20.6 282.5 %shard_map.118 = (bf16[1024,1280]{1,0:T(8,128)(2,1)}, bf16[1280,640]{1,0:T(8,128)(2,1)}) custom-call(bf16[1024,5120]{1,0:T(8,128)(2,1)} %tokens.1, bf16[640,1280]{1,0:T(8,128)(2,1)} %w_query.1, bf16[640,512]{1,0:T(8,128)(2,1)} %reshape.160.w_keyval, bf16[1280,640]{1,0:T(8,128)(2,1)} %w_out.1, bf16[2,8,128,256]{3,2,1,0:T(8,128)(2,1)} %bitcast_select_fusion.outgoing, ...), custom_call_target="tpu_custom_call" | custom-call | tf_op jit(solution)/shard_map/pallas_call | solution.py:800
  303.1 3.4 %copy.25 = bf16[1024,1280]{1,0:T(8,128)(2,1)} copy(bf16[1024,1280]{1,0:T(8,128)(2,1)} %get-tuple-element.7) | data formatting | bytes 5242880
  (12 shorter events, 0.1 us)
Async XLA Ops:
  0.0 4.1 %copy-start = (s32[8,16]{1,0:T(8,128)S(1)}, s32[8,16]{1,0:T(8,128)}, u32[]{:S(2)}) copy-start(s32[8,16]{1,0:T(8,128)} %param.23) | copy-start | bytes 1540
where the time goes:
time: 307 us
  Pallas kernels  282 us (92%)
  local copies, waits for them, and re-layouts  15.4 us (5%)
  other arithmetic  7.83 us (3%)
    pallas_call x1, Pallas kernels, fused_layer(): pl.pallas_call(fused_kernel, in_specs=[any_spec] * 5 + [vmem] * 5, out_sp...  282 us

commit v1 on v0

--- a/solution.py
+++ b/solution.py
@@ -340,8 +340,9 @@
     x_n = d + 2 - 4 * x_bit
     y_n = d + 4 - 8 * y_bit
     far = x_n + y_n - d
-    far_src = x_n + core * (y_n - x_n)
-    far_dst = y_n + core * (x_n - y_n)
+    flip = rem(m + core, 2)
+    far_src = x_n + flip * (y_n - x_n)
+    far_dst = y_n + flip * (x_n - y_n)
 
     def piece(k, owner):
         if isinstance(k, int) and k >= chunks:
@@ -399,11 +400,14 @@
             barrier, inc=1, device_id=(d, rem(m + s, planes)), device_id_type=MESH
         )
 
+    kv_at = [g + g * per_group * HD // TILE for g in range(kv_chunks)]
+
     def own_copy(k):
-        if k < kv_chunks:
-            source = w_keyval.at[:, pl.ds(k * TILE, TILE)]
+        if k in kv_at:
+            source = w_keyval.at[:, pl.ds(kv_at.index(k) * TILE, TILE)]
         else:
-            source = w_query.at[:, pl.ds((k - kv_chunks) * TILE, TILE)]
+            tile = k - sum(at < k for at in kv_at)
+            source = w_query.at[:, pl.ds(tile * TILE, TILE)]
         return pltpu.make_async_copy(source, piece(k, d), own_sem.at[k])
 
     for k in range(chunks):
@@ -431,6 +435,45 @@
             device_id_type=MESH,
         )
 
+    odd = rem(m, 2)
+    side = div(m, 2)
+    plane_to = 2 * rem(y_bit + flip, 2) + side
+
+    def swap_copy():
+        return pltpu.make_async_remote_copy(
+            src_ref=w_out,
+            dst_ref=relay,
+            send_sem=move_send.at[0],
+            recv_sem=move_recv.at[0],
+            device_id=(y_n, m),
+            device_id_type=MESH,
+        )
+
+    def lift_copy(source):
+        return pltpu.make_async_remote_copy(
+            src_ref=source,
+            dst_ref=wout.at[d],
+            send_sem=move_send.at[1],
+            recv_sem=move_recv.at[1],
+            device_id=(d, plane_to),
+            device_id_type=MESH,
+        )
+
+    def stay_copy(source):
+        return pltpu.make_async_copy(source, wout.at[d], move_recv.at[1])
+
+    @pl.when(flip == 1)
+    def _():
+        swap_copy().start()
+
+    @pl.when((flip == 0) & (plane_to == m))
+    def _():
+        stay_copy(w_out).start()
+
+    @pl.when((flip == 0) & (plane_to != m))
+    def _():
+        lift_copy(w_out).start()
+
     ahead = 3
     for k in range(ahead):
         own_copy(k).wait()
@@ -441,46 +484,6 @@
     for k in range(ahead, chunks):
         own_copy(k).wait()
 
-    odd = rem(m, 2)
-    side = div(m, 2)
-    upper = rem(y_bit + m, 2)
-    plane_to = 2 * upper + side
-
-    def swap_copy():
-        return pltpu.make_async_remote_copy(
-            src_ref=w_out,
-            dst_ref=relay,
-            send_sem=move_send.at[0],
-            recv_sem=move_recv.at[0],
-            device_id=(y_n, m),
-            device_id_type=MESH,
-        )
-
-    def lift_copy(source):
-        return pltpu.make_async_remote_copy(
-            src_ref=source,
-            dst_ref=wout.at[d],
-            send_sem=move_send.at[1],
-            recv_sem=move_recv.at[1],
-            device_id=(d, plane_to),
-            device_id_type=MESH,
-        )
-
-    def stay_copy(source):
-        return pltpu.make_async_copy(source, wout.at[d], move_recv.at[1])
-
-    @pl.when(odd == 1)
-    def _():
-        swap_copy().start()
-
-    @pl.when((odd == 0) & (plane_to == m))
-    def _():
-        stay_copy(w_out).start()
-
-    @pl.when((odd == 0) & (plane_to != m))
-    def _():
-        lift_copy(w_out).start()
-
     step_rows = 16
 
     def normalize(first, count):
@@ -496,23 +499,24 @@
     for b in range(blocks // 2):
         token_copy(b).wait()
         normalize(b * BLOCK, BLOCK)
+
+    @pl.when(flip == 1)
+    def _():
+        swap_copy().wait_recv()
+
+    @pl.when((flip == 1) & (plane_to == m))
+    def _():
+        stay_copy(relay).start()
+
+    @pl.when((flip == 1) & (plane_to != m))
+    def _():
+        lift_copy(relay).start()
+
     forward(0)
     issue(ahead)
     for b in range(blocks // 2, blocks):
         token_copy(b).wait()
         normalize(b * BLOCK, BLOCK)
-
-    @pl.when(odd == 1)
-    def _():
-        swap_copy().wait_recv()
-
-    @pl.when((odd == 1) & (plane_to == m))
-    def _():
-        stay_copy(relay).start()
-
-    @pl.when((odd == 1) & (plane_to != m))
-    def _():
-        lift_copy(relay).start()
 
     complete(0)
     forward(1)
@@ -533,19 +537,20 @@
             jnp.bfloat16
         )
 
+    second = kv_at[1] - 1
+
+    def chunk_of(t):
+        return t + 1 + div(t + second, 2 * second)
+
     def project_keyval(g):
         for first in (0, half_rows):
-            x = project(first, g)
+            x = project(first, kv_at[g])
             keys[first : first + half_rows, g * HD : (g + 1) * HD] = rotate(x[:, :HD], first)
             values[first : first + half_rows, g * HD : (g + 1) * HD] = x[:, HD:].astype(
                 jnp.bfloat16
             )
 
     project_keyval(0)
-    forward(2)
-    issue(ahead + 2)
-    complete(1)
-    project_keyval(1)
     for s in range(1, groups):
         page_copy(s).wait_recv()
     page_local.wait()
@@ -557,7 +562,7 @@
         return lax.dot_general(q, k, (((1,), (1,)), ((), ())), preferred_element_type=jnp.float32)
 
     def attend(first, t):
-        x = project(first, kv_chunks + t)
+        x = project(first, chunk_of(t))
         for j in range(2):
             query[:, j * HD : (j + 1) * HD] = rotate(x[:, j * HD : (j + 1) * HD], first)
 
@@ -640,8 +645,62 @@
                 att.at[part, columns], att_in.at[s, part, columns], z_recv.at[s, i]
             ).wait()
 
+    parts = range(chunks, chunks + out_parts)
+
+    def out_issue(block):
+        @pl.when(x_bit == block)
+        def _():
+            for k in parts:
+                issue(k)
+
+    def out_forward(block):
+        @pl.when(x_bit == block)
+        def _():
+            for k in parts:
+                hop(Y, k).wait_recv()
+
+                @pl.when(flip == 1)
+                def _():
+                    hop(FAR, k).start()
+
+                hop(OY, k).start()
+
+        @pl.when(x_bit != block)
+        def _():
+            for k in parts:
+                hop(X, k).wait_recv()
+
+                @pl.when(flip == 0)
+                def _():
+                    hop(FAR, k).start()
+
+                hop(OX, k).start()
+
+    def out_complete(block):
+        @pl.when(x_bit == block)
+        def _():
+            for k in parts:
+                hop(OWN, k).wait_recv()
+                hop(OY, k).wait_recv()
+
+        @pl.when(x_bit != block)
+        def _():
+            for k in parts:
+                hop(FAR, k).wait_recv()
+                hop(OFAR, k).start()
+            for k in parts:
+                hop(OX, k).wait_recv()
+                hop(OFAR, k).wait_recv()
+
     def tile_step(t, carry):
-        k = t + kv_chunks
+        k = chunk_of(t)
+
+        @pl.when(t == second)
+        def _():
+            forward(kv_at[1] + 1)
+            complete(kv_at[1])
+            project_keyval(1)
+
         complete(k)
         attend(0, t)
         z_start(t)
@@ -650,19 +709,14 @@
         def _():
             forward(k + 1)
 
-        @pl.when(t < tiles - 2)
-        def _():
-            issue_ahead = k + 2
-
-            @pl.when(issue_ahead >= 2 * ahead)
-            def _():
-                issue(issue_ahead)
+        @pl.when(t < chunks - ahead - 2)
+        def _():
+            issue(k + ahead + 1)
 
         @pl.when(t == tiles - 2)
         def _():
             stay_copy(relay).wait()
-            for part in range(out_parts):
-                issue(chunks + part)
+            out_issue(1 - odd)
 
         attend(half_rows, t)
         return carry
@@ -670,10 +724,9 @@
     lax.fori_loop(0, tiles, tile_step, 0)
     for i in range(tiles, tiles + blocks // 2):
         z_start(i)
-    for part in range(out_parts):
-        forward(chunks + part)
-    for part in range(out_parts):
-        complete(chunks + part)
+    out_forward(1 - odd)
+    out_issue(odd)
+    out_complete(1 - odd)
 
     partner = m + 1 - 2 * odd
 
@@ -691,8 +744,7 @@
     def head_partial(b, q, column_block):
         total = None
         for j in range(2):
-            order = j + side * 0 + upper_side * (1 - 2 * j)
-            index = order * (groups // 2) + column_block * 2 + q
+            index = rem(j + side + q, 2) * (groups // 2) + column_block * 2 + q
             term = jnp.dot(
                 att_in[j, b * BLOCK : (b + 1) * BLOCK, :],
                 wout[index],
@@ -700,8 +752,6 @@
             )
             total = term if total is None else total + term
         return total
-
-    upper_side = div(m, 2)
 
     def send_partial(b):
         for q in range(2):
@@ -732,6 +782,8 @@
         z_wait(i)
     for b in range(blocks // 2):
         send_partial(b)
+    out_forward(odd)
+    out_complete(odd)
     for b in range(blocks // 2, blocks):
         z_wait(tiles + b - blocks // 2)
         send_partial(b)
@@ -744,7 +796,7 @@
     for s in range(1, groups):
         page_copy(s).wait_send()
 
-    @pl.when(odd == 1)
+    @pl.when(flip == 1)
     def _():
         swap_copy().wait_send()
 
@@ -786,7 +838,14 @@
         return jnp.swapaxes(x.reshape(x.shape[0], 2, kv_local, HD), 1, 2).reshape(x.shape[0], -1)
 
     w_keyval = interleave(keyvalue_weight)
-    bias_row = jnp.concatenate([interleave(b_keyval[None])[0], b_query]).astype(jnp.float32)[None]
+    b_pair = interleave(b_keyval[None])[0]
+    pieces = []
+    per_group = q_width // HD // kv_local
+    for g in range(kv_local):
+        begin, end = ((g + i) * per_group * HD // (2 * HD) * 2 * HD for i in range(2))
+        end = q_width if g == kv_local - 1 else end
+        pieces += [b_pair[g * 2 * HD : (g + 1) * 2 * HD], b_query[begin:end]]
+    bias_row = jnp.concatenate(pieces).astype(jnp.float32)[None]
     gain = norm_gain.astype(jnp.float32)[None]
     any_spec = pl.BlockSpec(memory_space=pl.ANY)
     vmem = pl.BlockSpec(memory_space=pltpu.VMEM)
@@ -843,24 +902,29 @@
     page_len = kv_pool.shape[2]
     max_pages = page_owner.shape[1]
     group_ids = jnp.arange(groups, dtype=jnp.int32)
-    slot_prompt = jnp.sum(
-        jnp.where(prompt_device[None, :] == group_ids[:, None], group_ids[None, :], 0), axis=1
-    )
-    owners_all = jnp.take(page_owner, slot_prompt, axis=0)
-    index_all = jnp.take(page_index, slot_prompt, axis=0)
-    length_all = jnp.take(prefix_pages, slot_prompt, axis=0)
+    chosen_prompt = prompt_device[None, :] == group_ids[:, None]
+
+    def by_slot(table):
+        pick = chosen_prompt.reshape(chosen_prompt.shape + (1,) * (table.ndim - 1))
+        return jnp.sum(jnp.where(pick, table[None], 0), axis=1)
+
+    def of_mine(table):
+        pick = (prompt_device == my_group).reshape((-1,) + (1,) * (table.ndim - 1))
+        return jnp.sum(jnp.where(pick, table, 0), axis=0)
+
     slot_ids = jnp.arange(max_pages, dtype=jnp.int32)
     places = jnp.arange(CAP, dtype=jnp.int32)
-    used = slot_ids[None, :] < length_all[:, None]
-    mine = used & (owners_all == my_group)
-    rank = jnp.cumsum(mine.astype(jnp.int32), axis=1) - 1
+    used = slot_ids[None, :] < by_slot(prefix_pages)[:, None]
+    mine = used & (by_slot(page_owner) == my_group)
+    earlier = slot_ids[None, :] <= slot_ids[:, None]
+    rank = jnp.sum((mine[:, None, :] & earlier[None]).astype(jnp.int32), axis=2) - 1
     chosen = mine[:, None, :] & (rank[:, None, :] == places[None, :, None])
-    send_index = jnp.sum(jnp.where(chosen, index_all[:, None, :], 0), axis=2)
-    outgoing = jnp.take(kv_pool, send_index.reshape(-1), axis=1).reshape(
+    send_index = jnp.sum(jnp.where(chosen, by_slot(page_index)[:, None, :], 0), axis=2)
+    outgoing = kv_pool.at[:, send_index.reshape(-1)].get(mode="promise_in_bounds").reshape(
         2, groups, CAP, page_len, width_kv
     )
-    my_owners = jnp.take(owners_all, my_group, axis=0)
-    my_length = jnp.take(length_all, my_group, axis=0)
+    my_owners = of_mine(page_owner)
+    my_length = of_mine(prefix_pages)
     my_used = slot_ids < my_length
     counts = jnp.sum(
         ((my_owners[None, :] == group_ids[:, None]) & my_used[None, :]).astype(jnp.int32), axis=1

time: 307 us -> 277 us (0.902)
  the two profiles are of different devices: /device:TPU:24 before, /device:TPU:0 now
where the time goes in v1:
time: 277 us; the launch traced here: 276 us
  Pallas kernels  251 us (91%)
  local copies, waits for them, and re-layouts  13.1 us (5%)
  other arithmetic  10.8 us (4%)
    pallas_call x1, Pallas kernels, fused_layer(): pl.pallas_call(fused_kernel, in_specs=[any_spec] * 5 + [vmem] * 5, out_sp...  251 us

profile of v1, /device:TPU:0, one launch (start us, length us, event | category | flops | bytes accessed | tf_op | source)
XLA Modules:
  0.0 275.9 jit_solution(5966566000980565305)
XLA Ops:
  0.0 0.8 select_reduce_fusion.4
  0.8 0.7 slice.15
  1.5 0.7 iota_compare_fusion.4
  2.2 0.7 slice_bitcast_fusion.1
  2.8 1.3 select_reduce_fusion.5
  4.8 0.8 select_reduce_fusion.3
  5.6 0.6 iota_compare_fusion.6
  6.2 0.1 convert_reduce_fusion.1
  6.3 0.7 slice.17
  7.0 0.6 maximum_convert_fusion.bias
  7.7 0.1 fusion.3
  7.7 0.1 select_n.59
  7.8 0.8 select_reduce_fusion.1
  8.6 0.1 fusion.2
  8.7 0.2 convert_reduce_fusion
  8.9 0.1 select_reduce_fusion.2
  9.1 0.1 copy.20
  9.2 0.1 reshape.197
  9.3 0.1 broadcast_in_dim.125
  9.3 0.7 select_n.60.mask
  10.0 1.3 broadcast_in_dim.126
  11.3 2.8 %reshape.196.w_keyval = bf16[640,512]{1,0:T(8,128)(2,1)} reshape(bf16[640,2,2,128]{3,2,1,0:T(2,128)(2,1)} %bitcast.23) | data formatting | bytes 1310720 | tf_op jit(solution)/shard_map/reshape | solution.py:838
  14.2 2.8 %gather_fusion = bf16[16,2,64,256]{3,2,1,0:T(8,128)(2,1)S(1)} fusion(bf16[2,64,64,256]{3,2,1,0:T(8,128)(2,1)} %param.19, s32[1024]{0:T(1024)S(1)} %pad_clamp_fusion), kind=kCustom, calls=%fused_computation | custom fusion | bytes 2097216 | tf_op jit(solution)/shard_map/gather | solution.py:923
  17.0 1.0 copy.21
  18.0 1.9 fusion
  19.9 1.3 pad_maximum_fusion
  21.2 251.2 %shard_map.118 = (bf16[1024,1280]{1,0:T(8,128)(2,1)}, bf16[1280,640]{1,0:T(8,128)(2,1)}) custom-call(bf16[1024,5120]{1,0:T(8,128)(2,1)} %tokens.1, bf16[640,1280]{1,0:T(8,128)(2,1)} %w_query.1, bf16[640,512]{1,0:T(8,128)(2,1)} %reshape.196.w_keyval, bf16[1280,640]{1,0:T(8,128)(2,1)} %w_out.1, bf16[2,8,128,256]{3,2,1,0:T(8,128)(2,1)} %bitcast.22, ...), custom_call_target="tpu_custom_call" | custom-call | tf_op jit(solution)/shard_map/pallas_call | solution.py:859
  272.5 3.4 %copy.28 = bf16[1024,1280]{1,0:T(8,128)(2,1)} copy(bf16[1024,1280]{1,0:T(8,128)(2,1)} %get-tuple-element.6) | data formatting | bytes 5242880
  (9 shorter events, 0.1 us)

commit v2 on v1

--- a/solution.py
+++ b/solution.py
@@ -783,8 +783,9 @@
     for b in range(blocks // 2):
         send_partial(b)
     out_forward(odd)
-    out_complete(odd)
     for b in range(blocks // 2, blocks):
+        if b == blocks - 1:
+            out_complete(odd)
         z_wait(tiles + b - blocks // 2)
         send_partial(b)
     for b in range(blocks):
@@ -926,11 +927,11 @@
     my_owners = of_mine(page_owner)
     my_length = of_mine(prefix_pages)
     my_used = slot_ids < my_length
-    counts = jnp.sum(
-        ((my_owners[None, :] == group_ids[:, None]) & my_used[None, :]).astype(jnp.int32), axis=1
-    )
-    page_live = (places[None, :] < counts[:, None]).reshape(-1)
-    bias = jnp.where(jnp.repeat(page_live, page_len), 0.0, masked_score).astype(jnp.float32)[None]
+    key_ids = jnp.arange(groups * CAP * page_len, dtype=jnp.int32)
+    same = my_owners[None, :] == (key_ids // (CAP * page_len))[:, None]
+    count = jnp.sum((same & my_used[None, :]).astype(jnp.int32), axis=1)
+    live = (key_ids // page_len) % CAP < count
+    bias = jnp.where(live, 0.0, masked_score).astype(jnp.float32)[None]
     return outgoing, bias, my_length
 
 

time: 277 us -> 270 us (0.975)
  Pallas kernels: 251 us -> 245 us
    pallas_call x1, Pallas kernels: 251 us -> 245 us  [fused_layer(): pl.pallas_call(fused_kernel, in_specs=[any_spec] * 5 + [vmem] * 5, out_sp...]
where the time goes in v2:
time: 270 us; the launch traced here: 269 us
  Pallas kernels  245 us (91%)
  local copies, waits for them, and re-layouts  12.3 us (5%)
  other arithmetic  11.3 us (4%)
    pallas_call x1, Pallas kernels, fused_layer(): pl.pallas_call(fused_kernel, in_specs=[any_spec] * 5 + [vmem] * 5, out_sp...  245 us

profile of v2, /device:TPU:0, one launch (start us, length us, event | category | flops | bytes accessed | tf_op | source)
XLA Modules:
  0.0 269.4 jit_solution(14781131143015513648)
XLA Ops:
  0.0 0.8 select_reduce_fusion.4
  0.8 0.7 slice.15
  1.5 0.7 iota_compare_fusion.2
  2.2 0.7 slice_bitcast_fusion.1
  2.8 1.3 select_reduce_fusion.5
  4.8 0.8 select_reduce_fusion.3
  5.6 0.6 iota_compare_fusion.4
  6.2 0.7 slice.17
  6.9 0.6 maximum_convert_fusion.bias
  7.6 0.1 convert_reduce_fusion
  7.6 0.6 compare_select_fusion.2.mask
  8.2 0.8 select_reduce_fusion.1
  9.0 0.1 fusion.5
  9.1 0.2 convert_reduce_fusion.1
  9.4 0.1 select_reduce_fusion.2
  9.5 0.1 copy.20
  9.6 0.1 reshape.265
  9.7 1.3 broadcast_in_dim.120
  11.0 2.8 %reshape.264.w_keyval = bf16[640,512]{1,0:T(8,128)(2,1)} reshape(bf16[640,2,2,128]{3,2,1,0:T(2,128)(2,1)} %bitcast.24) | data formatting | bytes 1310720 | tf_op jit(solution)/shard_map/reshape | solution.py:839
  13.9 2.8 %gather_fusion = bf16[16,2,64,256]{3,2,1,0:T(8,128)(2,1)S(1)} fusion(bf16[2,64,64,256]{3,2,1,0:T(8,128)(2,1)} %param.19, s32[1024]{0:T(1024)S(1)} %pad_clamp_fusion), kind=kCustom, calls=%fused_computation | custom fusion | bytes 2097216 | tf_op jit(solution)/shard_map/gather | solution.py:924
  16.7 1.0 copy.21
  17.7 1.9 fusion
  19.6 1.3 pad_maximum_fusion
  20.9 245.0 %shard_map.118 = (bf16[1024,1280]{1,0:T(8,128)(2,1)}, bf16[1280,640]{1,0:T(8,128)(2,1)}) custom-call(bf16[1024,5120]{1,0:T(8,128)(2,1)} %tokens.1, bf16[640,1280]{1,0:T(8,128)(2,1)} %w_query.1, bf16[640,512]{1,0:T(8,128)(2,1)} %reshape.264.w_keyval, bf16[1280,640]{1,0:T(8,128)(2,1)} %w_out.1, bf16[2,8,128,256]{3,2,1,0:T(8,128)(2,1)} %bitcast.23, ...), custom_call_target="tpu_custom_call" | custom-call | tf_op jit(solution)/shard_map/pallas_call | solution.py:860
  266.0 3.4 %copy.28 = bf16[1024,1280]{1,0:T(8,128)(2,1)} copy(bf16[1024,1280]{1,0:T(8,128)(2,1)} %get-tuple-element.6) | data formatting | bytes 5242880
  (10 shorter events, 0.1 us)
